TPU v7x, 32 devices: a whole 2x2x4 slice. The times are simulated.
32 devices in a mesh: wide: 8 (over z, y), narrow: 4 (over x, core).
Axes of the slice: x: 2, y: 2, z: 4, core: 2. Of those that a mesh axis runs over, the one named last changes fastest.
Arguments:
- activations: bfloat16 [256, 28672], P('wide', 'narrow'), may hold values from -6 to 6
- out_grads: bfloat16 [256, 8192], P('wide'), may hold values from -6 to 6
- basis_in: bfloat16 [28672, 28672], P('narrow', 'wide'), may hold values from -0.03125 to 0.03125
- basis_out: bfloat16 [8192, 8192], P('wide', 'narrow'), may hold values from -0.0625 to 0.0625
- eigenvalues: bfloat16 [8192, 28672], P('narrow', 'wide'), may hold values from 0.29882812 to 10
- queries: bfloat16 [2, 8192, 28672], P(None, 'narrow', 'wide'), may hold values from -0.00036621094 to 0.00036621094
- doc_ids: int32 [256], replicated, may hold values from 0 to 15, never falling along the last dimension, each value on 1 to 32 neighbouring positions
Outputs:
- scores: float32 [16, 2], replicated
Inputs may be any that keep to these rules, and one draw needn't show every extreme that they name: `doc_ids`: document numbers never fall along the tokens; each document has 1 to 32 tokens.
All inputs are finite; a program needn't handle non-finite values.
Results may differ from a plain program's by a relative error of at most 0.0051.
Values may be sent and summed in bfloat16 or wider, within the bound.
A program may use at most 192 MiB of HBM per device.

v0:
```python
import jax
import jax.numpy as jnp
from jax import lax
from jax.sharding import PartitionSpec as P

DOC_PER = 2
DAMPING = 0.1


def shards(activations, out_grads, basis_in, basis_out, eigenvalues, queries, doc_ids):
    partial_acts = jnp.dot(
        lax.all_gather(activations, "wide", axis=0, tiled=True),
        basis_in,
        preferred_element_type=jnp.float32,
    )
    rot_acts = lax.psum(partial_acts, "narrow").astype(jnp.bfloat16)
    rows_held = lax.all_to_all(out_grads, "wide", split_axis=1, concat_axis=0, tiled=True)
    partial_grads = jnp.dot(rows_held, basis_out, preferred_element_type=jnp.float32)
    rot_grads = lax.psum(partial_grads, "wide").astype(jnp.bfloat16)
    precond = (
        queries.astype(jnp.float32) / (eigenvalues.astype(jnp.float32)[None] + DAMPING)
    ).astype(jnp.bfloat16)
    mixed_rows = jnp.einsum("ti,qij->qtj", rot_grads, precond, preferred_element_type=jnp.float32)
    token_part = jnp.sum(mixed_rows * rot_acts.astype(jnp.float32)[None], axis=2)
    doc_count = DOC_PER * lax.axis_size("wide")
    member = (doc_ids[None, :] == jnp.arange(doc_count, dtype=jnp.int32)[:, None]).astype(
        jnp.float32
    )
    partial_docs = jnp.dot(member, token_part.T, precision=lax.Precision.HIGHEST)
    return lax.psum(partial_docs, ("wide", "narrow"))


def solution(mesh):
    return jax.shard_map(
        shards,
        mesh=mesh,
        in_specs=(
            P("wide", "narrow"),
            P("wide", None),
            P("narrow", "wide"),
            P("wide", "narrow"),
            P("narrow", "wide"),
            P(None, "narrow", "wide"),
            P(),
        ),
        out_specs=P(),
        check_vma=False,
    )
```

profile of v0, /device:TPU:12, one launch (start us, length us, event | category | flops | bytes accessed | tf_op | source)
XLA Modules:
  0.0 313.9 jit_solution(6194928226690925329)
XLA Ops:
  6.5 0.0 all-gather.2.cloned.1.call-start
  6.5 0.7 all-gather.2.cloned.1.call-update
  7.3 1.9 copy.17
  9.1 6.2 %all-to-all-start = ((bf16[32,8,1024]{2,0,1:T(8,128)(2,1)}), bf16[32,8,1024]{2,0,1:T(8,128)(2,1)S(1)}, u32[]{:S(2)}, u32[]{:S(2)}) async-start(bf16[32,8,1024]{2,0,1:T(8,128)(2,1)} %bitcast.18), calls=%async_computation | async-start | bytes 1048576 | tf_op jit(solution)/shard_map/all_to_all | solution.py:17
  15.4 16.9 %convert_add_fusion = f32[2048,3584]{1,0:T(8,128)} fusion(bf16[2048,3584]{1,0:T(8,128)(2,1)} %param.11), kind=kLoop, calls=%fused_computation.1 | loop fusion | flops 14680064 | bytes 44040192 | tf_op jit(solution)/shard_map/add | solution.py:21
  32.2 3.7 %all-to-all-done = bf16[32,8,1024]{2,0,1:T(8,128)(2,1)S(1)} async-done(((bf16[32,8,1024]{2,0,1:T(8,128)(2,1)}), bf16[32,8,1024]{2,0,1:T(8,128)(2,1)S(1)}, u32[]{:S(2)}, u32[]{:S(2)}) %all-to-all-start) | async-done | bytes 524320 | tf_op jit(solution)/shard_map/all_to_all | solution.py:17
  35.9 3.5 %fusion.6 = f32[256,2048]{1,0:T(8,128)S(1)} fusion(bf16[256,1024]{1,0:T(8,128)(2,1)S(1)} %bitcast.20, bf16[1024,2048]{1,0:T(8,128)(2,1)} %param.10), kind=kOutput, calls=%fused_computation.12 | convolution fusion | flops 1073741824 | bytes 6815744 | tf_op jit(solution)/shard_map/dot_general | solution.py:18
  39.4 109.0 %all-reduce.3 = bf16[256,2048]{1,0:T(8,128)(2,1)S(1)} all-reduce(f32[256,2048]{1,0:T(8,128)S(1)} %fusion.6), channel_id=1, replica_groups=mesh['wide'=8,'narrow'=4] {'wide'}, use_global_device_ids=true, to_apply=%region_0.0 | all-reduce | flops 524288 | bytes 3145728 | tf_op jit(solution)/shard_map/psum | solution.py:19
  148.4 0.0 all-gather.2.cloned.1.call-done
  148.4 24.1 %fusion.7 = f32[256,3584]{1,0:T(8,128)} fusion(bf16[256,7168]{1,0:T(8,128)(2,1)} %all-gather.2.cloned.1.call-done, bf16[7168,3584]{1,0:T(8,128)(2,1)} %param.9), kind=kOutput, calls=%fused_computation.13 | convolution fusion | flops 13153337344 | bytes 58720256 | tf_op jit(solution)/shard_map/dot_general | solution.py:11
  172.5 67.2 %all-reduce.2 = bf16[256,3584]{1,0:T(8,128)(2,1)S(1)} all-reduce(f32[256,3584]{1,0:T(8,128)} %fusion.7), channel_id=1, replica_groups=mesh['wide'=8,'narrow'=4] {'narrow'}, use_global_device_ids=true, to_apply=%region_1.0 | all-reduce | flops 917504 | bytes 5505024 | tf_op jit(solution)/shard_map/psum | solution.py:16
  239.7 2.8 copy.13
  242.5 0.0 copy-start
  242.5 21.5 %fusion.1 = f32[2,256]{1,0:T(2,128)S(1)} fusion(bf16[2,2048,3584]{2,1,0:T(8,128)(2,1)} %param.12, f32[2048,3584]{1,0:T(8,128)} %convert_add_fusion, f32[256,3584]{0,1:T(8,128)} %copy.13, bf16[256,2048]{1,0:T(8,128)(2,1)S(1)} %all-reduce.3), kind=kOutput, calls=%fused_computation.4 | convolution fusion | flops 7563902464 | bytes 63440896 | tf_op jit(solution)/shard_map/ti,qij->qtj/dot_general | solution.py:23
  264.0 0.0 copy-done
  264.0 0.1 fusion.4
  264.1 42.9 %psum.23 = f32[16,2]{0,1:T(2,128)} all-reduce(f32[16,2]{0,1:T(2,128)S(1)} %fusion.4), channel_id=1, replica_groups=mesh['wide'=8,'narrow'=4] {'wide','narrow'}, use_global_device_ids=true, to_apply=%region_3.0 | all-reduce | flops 32 | bytes 256 | tf_op jit(solution)/shard_map/psum | solution.py:30
Async XLA Ops:
  6.5 141.9 %all-gather.2.cloned.1.call-start = ((), (), s32[]{:S(2)}) async-start(), calls=%async_computation.1 | async-start | bytes 4128768 | tf_op jit(solution)/shard_map/all_gather | solution.py:12
  9.1 26.8 %all-to-all-start = ((bf16[32,8,1024]{2,0,1:T(8,128)(2,1)}), bf16[32,8,1024]{2,0,1:T(8,128)(2,1)S(1)}, u32[]{:S(2)}, u32[]{:S(2)}) async-start(bf16[32,8,1024]{2,0,1:T(8,128)(2,1)} %bitcast.18), calls=%async_computation | async-start | bytes 1048576 | tf_op jit(solution)/shard_map/all_to_all | solution.py:17
  242.5 21.5 %copy-start = (s32[256]{0:T(256)S(1)}, s32[256]{0:T(256)}, u32[]{:S(2)}) copy-start(s32[256]{0:T(256)} %param.13) | copy-start | bytes 3076
Sparse Core Ops, SparseCore 0:
  9.5 117.3 all-gather.1
where the time goes:
time: 314 us
  blocking collectives  219 us (70%)
  matrix products  49.2 us (16%)
  other arithmetic  16.9 us (5%)
  between operations  13.4 us (4%)
  starting transfers between devices  6.22 us (2%)
  local copies, waits for them, and re-layouts  4.67 us (1%)
  waiting for transfers between devices  4.44 us (1%)
    psum x1, blocking collectives, shards(): rot_grads = lax.psum(partial_grads, 'wide').astype(jnp.bfloat16)  109 us
    psum x1, blocking collectives, shards(): rot_acts = lax.psum(partial_acts, 'narrow').astype(jnp.bfloat16)  67.2 us
    psum x1, blocking collectives, shards(): return lax.psum(partial_docs, ('wide', 'narrow'))  42.9 us
    dot_general x1, matrix products, shards(): jnp.dot(lax.all_gather(activations, 'wide', axis=0, tiled=True), basis_in...  24.1 us
    dot_general x1, matrix products, shards(): jnp.einsum('ti,qij->qtj', rot_grads, precond, preferred_element_type=jnp....  21.5 us
    add x1, other arithmetic, shards(): eigenvalues.astype(jnp.float32)[None] + DAMPING  16.9 us
  transfers between devices with their start and end apart: 2, of which 1 were waited for; matrix products, arithmetic and copies ran while one was open for 7% of the time, Pallas kernels for 0%

commit v1 on v0

--- a/solution.py
+++ b/solution.py
@@ -13,7 +13,7 @@
         basis_in,
         preferred_element_type=jnp.float32,
     )
-    rot_acts = lax.psum(partial_acts, "narrow").astype(jnp.bfloat16)
+    rot_acts = jnp.sum(lax.all_gather(partial_acts, "narrow"), axis=0).astype(jnp.bfloat16)
     rows_held = lax.all_to_all(out_grads, "wide", split_axis=1, concat_axis=0, tiled=True)
     partial_grads = jnp.dot(rows_held, basis_out, preferred_element_type=jnp.float32)
     rot_grads = lax.psum(partial_grads, "wide").astype(jnp.bfloat16)

time: 314 us -> 297 us (0.946)
  blocking collectives: 219 us -> 131 us
  waiting for transfers between devices: 4.44 us -> 69.3 us
  other arithmetic: 16.9 us -> 24.6 us
    all_gather x1, waiting for transfers between devices: 0.02 us -> 68.6 us  [shards(): lax.all_gather(activations, 'wide', axis=0, tiled=True)]
    psum x1 -> x0, blocking collectives: 67.2 us -> none  [shards(): rot_acts = lax.psum(partial_acts, 'narrow').astype(jnp.bfloat16)]
    psum x1, blocking collectives: 109 us -> 89.9 us  [shards(): rot_grads = lax.psum(partial_grads, 'wide').astype(jnp.bfloat16)]
    reduce_sum x0 -> x1, other arithmetic: none -> 7.11 us  [shards(): jnp.sum(lax.all_gather(partial_acts, 'narrow'), axis=0).astype(jnp.bfloat16)]
    all_to_all x1, waiting for transfers between devices: 3.71 us -> 0.01 us  [shards(): lax.all_to_all(out_grads, 'wide', split_axis=1, concat_axis=0, tiled=True)]
  transfers between devices with their start and end apart: 2 -> 3, of which waited for: 1 -> 1; matrix products, arithmetic and copies ran while one was open for 7% -> 7% of each run, Pallas kernels for 0% -> 0%
where the time goes in v1:
time: 297 us; the launch traced here: 296 us
  blocking collectives  131 us (44%)
  waiting for transfers between devices  69.3 us (23%)
  matrix products  49.4 us (17%)
  other arithmetic  24.6 us (8%)
  between operations  13.5 us (5%)
  starting transfers between devices  4.94 us (2%)
  local copies, waits for them, and re-layouts  3.65 us (1%)
    psum x1, blocking collectives, shards(): rot_grads = lax.psum(partial_grads, 'wide').astype(jnp.bfloat16)  89.9 us
    all_gather x1, waiting for transfers between devices, shards(): lax.all_gather(activations, 'wide', axis=0, tiled=True)  68.6 us
    psum x1, blocking collectives, shards(): return lax.psum(partial_docs, ('wide', 'narrow'))  40.9 us
    dot_general x1, matrix products, shards(): jnp.dot(lax.all_gather(activations, 'wide', axis=0, tiled=True), basis_in...  24.2 us
    dot_general x1, matrix products, shards(): jnp.einsum('ti,qij->qtj', rot_grads, precond, preferred_element_type=jnp....  21.5 us
    add x1, other arithmetic, shards(): eigenvalues.astype(jnp.float32)[None] + DAMPING  17.5 us
    reduce_sum x1, other arithmetic, shards(): jnp.sum(lax.all_gather(partial_acts, 'narrow'), axis=0).astype(jnp.bfloat16)  7.11 us
  transfers between devices with their start and end apart: 3, of which 1 were waited for; matrix products, arithmetic and copies ran while one was open for 7% of the time, Pallas kernels for 0%

profile of v1, /device:TPU:12, one launch (start us, length us, event | category | flops | bytes accessed | tf_op | source)
XLA Modules:
  0.0 296.3 jit_solution(11618665509272139795)
XLA Ops:
  6.5 0.0 all-gather.4.cloned.1.call-start
  6.5 0.7 all-gather.4.cloned.1.call-update
  7.3 0.0 copy-start
  7.3 0.0 all-gather.6.cloned.1.call-start
  7.3 68.6 %all-gather.4.cloned.1.call-done = bf16[256,7168]{1,0:T(8,128)(2,1)} async-done(((bf16[32,7168]{1,0:T(8,128)(2,1)}), bf16[256,7168]{1,0:T(8,128)(2,1)}) %all-gather.4.cloned.1.call-update) | async-done | bytes 3670032 | tf_op jit(solution)/shard_map/all_gather | solution.py:12
  75.9 24.2 %fusion.7 = f32[256,3584]{1,0:T(8,128)} fusion(bf16[256,7168]{1,0:T(8,128)(2,1)} %all-gather.4.cloned.1.call-done, bf16[7168,3584]{1,0:T(8,128)(2,1)} %param.9), kind=kOutput, calls=%fused_computation.13 | convolution fusion | flops 13153337344 | bytes 58720256 | tf_op jit(solution)/shard_map/dot_general | solution.py:11
  100.1 0.0 all-gather.6.cloned.1.call-update
  100.1 0.0 copy-done
  100.1 0.9 copy.16
  101.0 4.9 %all-to-all-start = ((bf16[32,8,1024]{2,0,1:T(8,128)(2,1)}), bf16[32,8,1024]{2,0,1:T(8,128)(2,1)S(1)}, u32[]{:S(2)}, u32[]{:S(2)}) async-start(bf16[32,8,1024]{2,0,1:T(8,128)(2,1)} %bitcast.19), calls=%async_computation | async-start | bytes 1048576 | tf_op jit(solution)/shard_map/all_to_all | solution.py:17
  105.9 17.5 %convert_add_fusion = f32[2048,3584]{1,0:T(8,128)} fusion(bf16[2048,3584]{1,0:T(8,128)(2,1)} %param.11), kind=kLoop, calls=%fused_computation.1 | loop fusion | flops 14680064 | bytes 44040192 | tf_op jit(solution)/shard_map/add | solution.py:21
  123.4 0.0 all-to-all-done
  123.4 3.6 %fusion.6 = f32[256,2048]{1,0:T(8,128)S(1)} fusion(bf16[256,1024]{1,0:T(8,128)(2,1)S(1)} %bitcast.22, bf16[1024,2048]{1,0:T(8,128)(2,1)} %param.10), kind=kOutput, calls=%fused_computation.12 | convolution fusion | flops 1073741824 | bytes 6815744 | tf_op jit(solution)/shard_map/dot_general | solution.py:18
  127.0 89.9 %all-reduce.1 = bf16[256,2048]{1,0:T(8,128)(2,1)S(1)} all-reduce(f32[256,2048]{1,0:T(8,128)S(1)} %fusion.6), channel_id=1, replica_groups=mesh['wide'=8,'narrow'=4] {'wide'}, use_global_device_ids=true, to_apply=%region_0.0 | all-reduce | flops 524288 | bytes 3145728 | tf_op jit(solution)/shard_map/psum | solution.py:19
  217.0 0.0 all-gather.6.cloned.1.call-done
  217.0 7.1 %reduce_sum.18 = bf16[256,3584]{1,0:T(8,128)(2,1)S(1)} reduce(f32[4,256,3584]{2,1,0:T(8,128)} %bitcast.20, f32[]{:T(128)} %constant.1.clone.1), dimensions={0}, to_apply=%region_1.0 | reduce | flops 2752512 | bytes 16515076 | tf_op jit(solution)/shard_map/reduce_sum | solution.py:16
  224.1 2.8 copy.12
  226.9 0.0 copy-start.1
  226.9 21.5 %fusion.1 = f32[2,256]{1,0:T(2,128)S(1)} fusion(bf16[2,2048,3584]{2,1,0:T(8,128)(2,1)} %param.12, f32[2048,3584]{1,0:T(8,128)} %convert_add_fusion, f32[256,3584]{0,1:T(8,128)} %copy.12, bf16[256,2048]{1,0:T(8,128)(2,1)S(1)} %all-reduce.1), kind=kOutput, calls=%fused_computation.4 | convolution fusion | flops 7563902464 | bytes 63440896 | tf_op jit(solution)/shard_map/ti,qij->qtj/dot_general | solution.py:23
  248.4 0.0 copy-done.1
  248.4 0.1 fusion.4
  248.5 40.9 %psum.15 = f32[16,2]{0,1:T(2,128)} all-reduce(f32[16,2]{0,1:T(2,128)S(1)} %fusion.4), channel_id=1, replica_groups=mesh['wide'=8,'narrow'=4] {'wide','narrow'}, use_global_device_ids=true, to_apply=%region_3.0 | all-reduce | flops 32 | bytes 256 | tf_op jit(solution)/shard_map/psum | solution.py:30
Async XLA Ops:
  6.5 69.4 %all-gather.4.cloned.1.call-start = ((), (), s32[]{:S(2)}) async-start(), calls=%async_computation.1 | async-start | bytes 4128768 | tf_op jit(solution)/shard_map/all_gather | solution.py:12
  7.3 92.9 %copy-start = (bf16[32,8192]{1,0:T(8,128)(2,1)S(1)}, bf16[32,8192]{1,0:T(8,128)(2,1)}, u32[]{:S(2)}) copy-start(bf16[32,8192]{1,0:T(8,128)(2,1)} %param.8) | copy-start | bytes 1572868
  7.3 209.7 %all-gather.6.cloned.1.call-start = ((), (), s32[]{:S(2)}) async-start(), calls=%async_computation.2 | async-start | bytes 18350080 | tf_op jit(solution)/shard_map/all_gather | solution.py:16
  101.0 22.4 %all-to-all-start = ((bf16[32,8,1024]{2,0,1:T(8,128)(2,1)}), bf16[32,8,1024]{2,0,1:T(8,128)(2,1)S(1)}, u32[]{:S(2)}, u32[]{:S(2)}) async-start(bf16[32,8,1024]{2,0,1:T(8,128)(2,1)} %bitcast.19), calls=%async_computation | async-start | bytes 1048576 | tf_op jit(solution)/shard_map/all_to_all | solution.py:17
  226.9 21.5 %copy-start.1 = (s32[256]{0:T(256)S(1)}, s32[256]{0:T(256)}, u32[]{:S(2)}) copy-start(s32[256]{0:T(256)} %param.13) | copy-start | bytes 3076
Sparse Core Ops, SparseCore 0:
  9.5 66.3 all-gather.3
  100.2 93.6 all-gather.5
